TPU v7x, 256 devices: a whole 4x4x8 slice. The times are simulated.
256 devices in a mesh: dp: 32 (over x, z_lo, core), mp: 8 (over y, z_hi).
Axes of the slice: x: 4, y: 4, z: 8 (z_hi: 2, z_lo: 4; z = z_hi * 4 + z_lo), core: 2. Of those that a mesh axis runs over, the one named last changes fastest.
Arguments:
- gradients: bfloat16 [32, 59392, 128], P('dp', 'mp'), may hold values from -8 to 8
- weights: float32 [59392, 128], P('mp'), may hold values from -40 to 40
- first_moment: float32 [8, 7424, 128], P('mp', 'dp'), may hold values from -240 to 240
- second_moment: float32 [8, 7424, 128], P('mp', 'dp'), may hold values from 0.3 to 3
- owner_list: int32 [8, 7424], P('mp'), may hold values from 0 to 31, as said below
- norm_grads: bfloat16 [32, 2, 1024], P('dp'), may hold values from -6 to 6
- norm_state: float32 [3, 2, 1024], replicated, may hold values from -1.6 to 3, as said below
Outputs:
- new_weights: float32 [59392, 128], P('mp')
- new_first: float32 [8, 7424, 128], P('mp', 'dp')
- new_second: float32 [8, 7424, 128], P('mp', 'dp')
- new_norm_state: float32 [3, 2, 1024], replicated
- trust_ratios: float32 [7], replicated
Inputs may be any that keep to these rules, and one draw needn't show every extreme that they name: `owner_list`: in every mp shard each dp index owns exactly 232 of the 7424 blocks. `norm_state`: gains near 1, second moments positive.
All inputs are finite; a program needn't handle non-finite values.
Results may differ from a plain program's by a relative error of at most 0.0003.
Values sent between devices are 32-bit elements; how exact they have to be, the bound alone decides.
A program may use at most 64 MiB of HBM per device.

v0:
```python
import jax
import jax.numpy as jnp
from jax import lax
from jax.sharding import PartitionSpec as P

D = 1024
NTAB = 8
NKEYS = 256
KDIM = 128
LANE = 128
VROW_DEV = 512


beta_one = 0.9
beta_two = 0.99
bias_one = 1.0 - 0.9**4
bias_two = 1.0 - 0.99**4
epsilon = 1e-06
learning = 0.02
decay_rate = 0.01
matrices = 5


def block_matrix(block_count, narrow):
    query_blocks = D * D // (LANE * narrow)
    key_blocks = NTAB * NKEYS * KDIM // (LANE * narrow)
    value_blocks = VROW_DEV * D // LANE
    position = jnp.arange(block_count, dtype=jnp.int32)
    bounds = (
        query_blocks,
        query_blocks + key_blocks,
        query_blocks + key_blocks + value_blocks,
        2 * query_blocks + key_blocks + value_blocks,
    )
    result = jnp.zeros((block_count,), jnp.int32)
    for boundary in bounds:
        result = result + (position >= boundary).astype(jnp.int32)
    return result


def adam_step(gradient, moment_one, moment_two, weight):
    moment_one = beta_one * moment_one + (1.0 - beta_one) * gradient
    moment_two = beta_two * moment_two + (1.0 - beta_two) * gradient * gradient
    update = (
        moment_one / bias_one / (jnp.sqrt(moment_two / bias_two) + epsilon) + decay_rate * weight
    )
    return (moment_one, moment_two, update)


def member_table(matrix_of):
    return (matrix_of[:, None] == jnp.arange(matrices, dtype=jnp.int32)[None, :]).astype(
        jnp.float32
    )


def local(gradients, weights, first_moment, second_moment, owner_list, norm_grads, norm_state):
    narrow = lax.axis_size("mp")
    replicas = lax.axis_size("dp")
    block_count = weights.shape[0]
    per_owner = block_count // replicas
    matrix_of = block_matrix(block_count, narrow)
    owner_order = jnp.argsort(owner_list[0], stable=True)
    local_grads = gradients[0]
    gradient = lax.psum_scatter(
        local_grads[owner_order].astype(jnp.float32), "dp", scatter_dimension=0, tiled=True
    )
    norm_sum = lax.psum(norm_grads[0].astype(jnp.float32), "dp")
    owned_rows = lax.dynamic_slice_in_dim(owner_order, lax.axis_index("dp") * per_owner, per_owner)
    weight_own = weights[owned_rows]
    member = member_table(matrix_of[owned_rows])
    moment_one, moment_two, update = adam_step(
        gradient, first_moment[0], second_moment[0], weight_own
    )
    position_of = jnp.argsort(owner_order)
    squares = jnp.stack(
        [jnp.sum(weight_own * weight_own, axis=1), jnp.sum(update * update, axis=1)]
    )
    totals = lax.psum(jnp.dot(squares, member, precision=lax.Precision.HIGHEST), ("dp", "mp"))
    weight_sq = totals[0]
    update_sq = totals[1]
    ratios = jnp.sqrt(weight_sq) / (jnp.sqrt(update_sq) + epsilon)
    row_rates = jnp.dot(member, ratios, precision=lax.Precision.HIGHEST)
    fresh_rows = weight_own - learning * row_rates[:, None] * update
    new_weights = lax.all_gather(fresh_rows, "dp", axis=0, tiled=True)[position_of]
    gain_rows = norm_state[0]
    norm_one, norm_two, norm_update = adam_step(norm_sum, norm_state[1], norm_state[2], gain_rows)
    norm_ratio = jnp.sqrt(jnp.sum(gain_rows * gain_rows, axis=1)) / (
        jnp.sqrt(jnp.sum(norm_update * norm_update, axis=1)) + epsilon
    )
    new_gains = gain_rows - learning * norm_ratio[:, None] * norm_update
    new_state = jnp.stack([new_gains, norm_one, norm_two])
    trust_ratios = jnp.concatenate([ratios, norm_ratio])
    return (new_weights, moment_one[None], moment_two[None], new_state, trust_ratios)


def solution(mesh):
    in_specs = (
        P("dp", "mp", None),
        P("mp", None),
        P("mp", "dp", None),
        P("mp", "dp", None),
        P("mp", None),
        P("dp", None, None),
        P(),
    )
    out_specs = (P("mp", None), P("mp", "dp", None), P("mp", "dp", None), P(), P())
    return jax.shard_map(local, mesh=mesh, in_specs=in_specs, out_specs=out_specs, check_vma=False)
```

profile of v0, /device:TPU:1, one launch (start us, length us, event | category | flops | bytes accessed | tf_op | source)
XLA Modules:
  0.0 369.0 jit_solution(8637664813541310505)
XLA Ops:
  7.2 0.0 reduce-scatter.5.cloned.1.call-start
  7.2 1.0 reduce
  8.2 6.6 %sort.34 = (s32[7424]{0:T(1024)}, s32[7424]{0:T(1024)S(1)}) sort(s32[7424]{0:T(1024)S(1)} %reduce, s32[7424]{0:T(1024)S(1)} %iota.15), dimensions={0}, to_apply=%region_0.0 | sort | flops 96512 | bytes 118784 | tf_op jit(solution)/shard_map/jit(argsort)/sort | solution.py:62
  14.9 15.7 %gather_fusion.2 = bf16[7424,128]{1,0:T(8,128)(2,1)} fusion(bf16[7424,128]{1,0:T(8,128)(2,1)S(1)} %bitcast.62, s32[8192]{0:T(1024)S(1)} %pad_clamp_fusion.1), kind=kCustom, calls=%fused_computation.2 | custom fusion | bytes 3830784 | tf_op jit(solution)/shard_map/gather | solution.py:65
  30.5 3.6 convert_element_type.26
  34.2 0.0 reduce-scatter.5.cloned.1.call-update
  34.2 0.0 all-gather.2.cloned.1.call-start
  34.3 0.1 compare_select_fusion.2
  34.4 2.8 gather_fusion
  37.2 1.7 gather_fusion.1
  38.9 145.8 %reduce-scatter.5.cloned.1.call-done = f32[232,128]{1,0:T(8,128)} async-done(((f32[7424,128]{1,0:T(8,128)}), f32[232,128]{1,0:T(8,128)}) %reduce-scatter.5.cloned.1.call-update) | async-done | bytes 118800
  184.8 1.7 multiply_reduce_fusion
  186.4 0.2 fusion.2
  186.6 80.9 %psum.14 = f32[2,5]{1,0:T(2,128)S(1)} all-reduce(f32[2,5]{1,0:T(2,128)S(1)} %fusion.2), channel_id=1, replica_groups=mesh['dp'=32,'mp'=8] {'dp','mp'}, use_global_device_ids=true, to_apply=%region_4.5 | all-reduce | flops 10 | bytes 80 | tf_op jit(solution)/shard_map/psum | solution.py:78
  267.5 0.2 fusion.1
  267.8 0.8 multiply_subtract_fusion
  268.6 0.0 all-gather.2.cloned.1.call-update
  268.6 6.6 %sort.35 = (s32[7424]{0:T(1024)}, s32[7424]{0:T(1024)S(1)}) sort(s32[7424]{0:T(1024)S(1)} %get-tuple-element.7, s32[7424]{0:T(1024)S(1)} %iota.17), dimensions={0}, to_apply=%region_5.6 | sort | flops 96512 | bytes 118784 | tf_op jit(solution)/shard_map/jit(argsort)/sort | solution.py:74
  275.3 68.9 %psum.15 = f32[2,1024]{1,0:T(2,128)S(1)} all-reduce(f32[2,1024]{1,0:T(2,128)S(1)} %bitcast_convert_fusion), channel_id=1, replica_groups=mesh['dp'=32,'mp'=8] {'dp'}, use_global_device_ids=true, to_apply=%region_7.8 | all-reduce | flops 2048 | bytes 16384 | tf_op jit(solution)/shard_map/psum | solution.py:67
  344.2 0.2 multiply_reduce_fusion.2
  344.4 0.1 fusion.10
  344.5 0.6 pad_maximum_fusion
  345.1 0.6 pad_maximum_fusion.1
  345.7 16.5 %gather_fusion.3 = f32[7424,128]{1,0:T(8,128)} fusion(f32[7424,128]{1,0:T(8,128)} %all-gather.2.cloned.1.call-done, s32[8192]{0:T(1024)S(1)} %pad_clamp_fusion), kind=kCustom, calls=%fused_computation.3 | custom fusion | bytes 7631872 | tf_op jit(solution)/shard_map/gather | solution.py:84
  (23 shorter events, 0.1 us)
Async XLA Ops:
  7.2 7.7 %copy-start = (bf16[1,7424,128]{2,1,0:T(8,128)(2,1)S(1)}, bf16[1,7424,128]{2,1,0:T(8,128)(2,1)}, u32[]{:S(2)}) copy-start(bf16[1,7424,128]{2,1,0:T(8,128)(2,1)} %param.7) | copy-start | bytes 5701636
  7.2 177.6 %reduce-scatter.5.cloned.1.call-start = ((), (), s32[]{:S(2)}) async-start(), calls=%async_computation.2 | async-start | bytes 3919872
  34.2 150.6 %copy-start.1 = (f32[1,232,128]{2,1,0:T(8,128)S(1)}, f32[1,232,128]{2,1,0:T(8,128)}, u32[]{:S(2)}) copy-start(f32[1,232,128]{2,1,0:T(8,128)} %param.10) | copy-start | bytes 356356
  34.2 150.6 %copy-start.2 = (f32[1,232,128]{2,1,0:T(8,128)S(1)}, f32[1,232,128]{2,1,0:T(8,128)}, u32[]{:S(2)}) copy-start(f32[1,232,128]{2,1,0:T(8,128)} %param.9) | copy-start | bytes 356356
  34.2 241.1 %copy-start.4 = (bf16[1,2,1024]{2,1,0:T(2,128)(2,1)S(1)}, bf16[1,2,1024]{2,1,0:T(2,128)(2,1)}, u32[]{:S(2)}) copy-start(bf16[1,2,1024]{2,1,0:T(2,128)(2,1)} %param.12) | copy-start | bytes 12292
  34.2 310.0 %copy-start.3 = (f32[3,2,1024]{2,1,0:T(2,128)S(1)}, f32[3,2,1024]{2,1,0:T(2,128)}, u32[]{:S(2)}) copy-start(f32[3,2,1024]{2,1,0:T(2,128)} %param.13) | copy-start | bytes 73732
  34.2 311.5 %all-gather.2.cloned.1.call-start = ((), (), s32[]{:S(2)}) async-start(), calls=%async_computation.1 | async-start | bytes 3919872 | tf_op jit(solution)/shard_map/all_gather | solution.py:84
Sparse Core Ops, SparseCore 0:
  34.4 150.3 reduce-scatter.4
  268.7 57.4 all-gather.1
where the time goes:
time: 369 us
  blocking collectives  150 us (41%)
  waiting for transfers between devices  146 us (40%)
  local copies, waits for them, and re-layouts  36.7 us (10%)
  other arithmetic  22 us (6%)
  between operations  14.1 us (4%)
    unnamed x3, waiting for transfers between devices  146 us
    psum x1, blocking collectives, local(): lax.psum(jnp.dot(squares, member, precision=lax.Precision.HIGHEST), ('dp'...  80.9 us
    psum x1, blocking collectives, local(): norm_sum = lax.psum(norm_grads[0].astype(jnp.float32), 'dp')  68.9 us
    gather x1, local copies, waits for them, and re-layouts, local(): lax.all_gather(fresh_rows, 'dp', axis=0, tiled=True)[position_of]  16.5 us
    gather x1, local copies, waits for them, and re-layouts, local(): local_grads[owner_order].astype(jnp.float32)  15.7 us
  transfers between devices with their start and end apart: 2, of which 1 were waited for; matrix products, arithmetic and copies ran while one was open for 3% of the time, Pallas kernels for 0%

commit v1 on v0

v1 whole, which is shorter than its diff:
```python
import functools

import jax
import jax.numpy as jnp
from jax import lax
from jax.experimental import pallas as pl
from jax.experimental.pallas import tpu as pltpu
from jax.sharding import PartitionSpec as P

LANE = 128
NX, NZ, NC, ZH = 4, 4, 2, 2
QUERY, KEYS, VALUES = 1024, 256, 4096
MATRICES = 5
RBLK = 256
RPAD = 256

beta_one = 0.9
beta_two = 0.99
bias_one = 1.0 - 0.9**4
bias_two = 1.0 - 0.99**4
epsilon = 1e-06
learning = 0.02
decay_rate = 0.01

MESH = pl.DeviceIdType.MESH
VMEM = pltpu.VMEM
SMEM = pltpu.SMEM
f32 = jnp.float32
bf16 = jnp.bfloat16
i32 = jnp.int32


def matrix_bounds():
    return (QUERY, QUERY + KEYS, QUERY + KEYS + VALUES, 2 * QUERY + KEYS + VALUES)


def adam_step(gradient, moment_one, moment_two, weight):
    moment_one = beta_one * moment_one + (1.0 - beta_one) * gradient
    moment_two = beta_two * moment_two + (1.0 - beta_two) * gradient * gradient
    update = (
        moment_one / bias_one / (jnp.sqrt(moment_two / bias_two) + epsilon) + decay_rate * weight
    )
    return moment_one, moment_two, update


def tables_kernel(n, owner_ref, out_ref, own_s, m_s, t_s, a_s, b_s):
    rows = owner_ref.shape[0]
    owners = NX * NZ * NC
    own_s[...] = jnp.full((64, LANE), 99, i32)
    own_s[0:rows, :] = owner_ref[...]
    own = own_s[...]
    for o in range(owners):
        m_s[o * 64 : (o + 1) * 64, :] = jnp.where(own == o, 1.0, 0.0).astype(bf16)
    r0 = lax.broadcasted_iota(i32, (LANE, 2 * LANE), 0)
    c0 = lax.broadcasted_iota(i32, (LANE, 2 * LANE), 1)
    upper = jnp.where(r0 < c0, 1.0, 0.0).astype(bf16)
    prefix = jnp.dot(m_s[...], upper, preferred_element_type=f32)
    for o in range(owners):
        t_s[:, o * LANE : (o + 1) * LANE] = prefix[o * 64 : (o + 1) * 64, LANE:].astype(bf16)
    r1 = lax.broadcasted_iota(i32, (64, 64), 0)
    c1 = lax.broadcasted_iota(i32, (64, 64), 1)
    lower = jnp.where(c1 < r1, 1.0, 0.0).astype(bf16)
    above = jnp.dot(lower, t_s[...], preferred_element_type=f32)
    rank = jnp.zeros((64, LANE), f32)
    for o in range(owners):
        here = prefix[o * 64 : (o + 1) * 64, :LANE] + above[:, o * LANE : (o + 1) * LANE]
        rank = rank + jnp.where(own == o, here, 0.0)
    out_ref[0:64, :] = own * n + rank.astype(i32)
    rank_i = rank.astype(i32)
    sub = lax.broadcasted_iota(i32, (RPAD, LANE), 0)
    dev = lax.broadcasted_iota(i32, (owners, LANE), 0)
    lane = lax.broadcasted_iota(i32, (owners, LANE), 1).astype(f32)
    for i in range(rows):
        b_s[:, i * LANE : (i + 1) * LANE] = jnp.where(rank_i[i : i + 1, :] == sub, 1.0, 0.0).astype(bf16)
        mine = own[i : i + 1, :] == dev
        a_s[0:owners, i * LANE : (i + 1) * LANE] = jnp.where(mine, float(i), 0.0).astype(bf16)
        a_s[owners:, i * LANE : (i + 1) * LANE] = jnp.where(mine, lane, 0.0).astype(bf16)
    found = lax.dot_general(
        a_s[...], b_s[...], (((1,), (1,)), ((), ())), preferred_element_type=f32
    )
    order = (found[0:owners] * float(LANE) + found[owners:]).astype(i32)
    out_ref[64:96, :] = order[:, :LANE]
    out_ref[96:128, :] = order[:, LANE:]


def tables(owner, n):
    rows = owner.shape[0]
    return pl.pallas_call(
        functools.partial(tables_kernel, n),
        out_shape=jax.ShapeDtypeStruct((128, LANE), i32),
        in_specs=[pl.BlockSpec(memory_space=VMEM)],
        out_specs=pl.BlockSpec(memory_space=VMEM),
        scratch_shapes=[
            VMEM((64, LANE), i32),
            VMEM((NX * NZ * NC * 64, LANE), bf16),
            VMEM((64, NX * NZ * NC * LANE), bf16),
            VMEM((64, rows * LANE), bf16),
            VMEM((RPAD, rows * LANE), bf16),
        ],
        name="owner_tables",
    )(owner)


def order_at(tab, d, r):
    return tab[(64 + (r // LANE) * 32) * LANE + d * LANE + r % LANE]


def permute_kernel(n, tab, g_ref, w_ref, out_ref, wown_ref, idx_ref, gf):
    total = g_ref.shape[0]
    step = 256

    def widen(i, carry):
        at = pl.ds(pl.multiple_of(i * step, step), step)
        gf[at, :] = g_ref[at, :].astype(f32)
        return carry

    lax.fori_loop(0, total // step, widen, 0)

    def one(d, carry):
        for r in range(n):
            out_ref[d, pl.ds(r, 1), :] = gf[pl.ds(order_at(tab, d, r), 1), :]
        return carry

    lax.fori_loop(0, NX * NZ * NC, one, 0)
    me = lax.axis_index("dp")
    for r in range(n):
        b = order_at(tab, me, r)
        wown_ref[pl.ds(r, 1), :] = w_ref[pl.ds(b, 1), :]
        idx_ref[pl.ds(r, 1), :] = jnp.full((1, LANE), b, i32)


def permute(tab, grads, weights, n):
    total = grads.shape[0]
    return pl.pallas_call(
        functools.partial(permute_kernel, n),
        out_shape=(
            jax.ShapeDtypeStruct((NX * NZ * NC, n, LANE), f32),
            jax.ShapeDtypeStruct((n, LANE), f32),
            jax.ShapeDtypeStruct((n, LANE), i32),
        ),
        in_specs=[
            pl.BlockSpec(memory_space=SMEM),
            pl.BlockSpec(memory_space=VMEM),
            pl.BlockSpec(memory_space=VMEM),
        ],
        out_specs=(pl.BlockSpec(memory_space=VMEM),) * 3,
        scratch_shapes=[VMEM((total, LANE), f32)],
        name="permute_rows",
    )(tab, grads, weights)


def exchange_kernel(
    n, half, ny,
    gp, m1, m2, wown, idx, ng,
    dall, m1n, m2n, stats, nsum,
    rbuf, col, x2p, x2m, left, right, zbuf, tot,
    nb1, nb2, sb1, sb2, sb3,
    ps, pr, xs, xr, zs, zr,
    ns1, nr1, ns2, nr2, ss1, sr1, ss2, sr2, ss3, sr3,
    gzs, gzr, gxs, gxr, gps, gpr,
):
    me = lax.axis_index("dp")
    m = lax.axis_index("mp")
    x = me // (NZ * NC)
    z = (me // NC) % NZ
    c = me % NC
    y = m // ZH
    zh = m % ZH
    ha = pl.ds(0, half)
    hb = pl.ds(half, n - half)

    def at(x_, z_, c_):
        return x_ * (NZ * NC) + z_ * NC + c_

    xp, xm, xo = (x + 1) % NX, (x + 3) % NX, (x + 2) % NX
    up = (z // 2) * 2 - 1
    zk = [(z + up * (1 + k) + 8) % NZ for k in range(NZ)]
    oc = 1 - c
    xc = x * NC + c
    xcp = [(xc + j) % (NX * NC) for j in range(1, NX * NC)]

    def dev(d):
        return (d, m)

    partner = dev(at(x, z, oc))
    xc_dev = [dev(at(p // NC, z, p % NC)) for p in xcp]
    z_dev = [dev(at(x, (z + j) % NZ, c)) for j in range(1, NZ)]
    zz = zh * NZ + z
    zzp = [(zz + j) % (ZH * NZ) for j in range(1, ZH * NZ)]
    zz_dev = [(at(x, p % NZ, c), y * ZH + p // NZ) for p in zzp]
    yp = [(y + j) % ny for j in range(1, ny)]
    y_dev = [(me, p * ZH + zh) for p in yp]

    barrier = pltpu.get_barrier_semaphore()
    peers = xc_dev + zz_dev + y_dev
    for peer in peers:
        pl.semaphore_signal(barrier, inc=1, device_id=peer, device_id_type=MESH)
    nb1[xc] = ng[...].astype(f32)
    pl.semaphore_wait(barrier, len(peers))

    def send(src, dst, ssem, rsem, to):
        copy = pltpu.make_async_remote_copy(
            src_ref=src, dst_ref=dst, send_sem=ssem, recv_sem=rsem,
            device_id=to, device_id_type=MESH,
        )
        copy.start()
        return copy

    def arrived(dst, rsem):
        pltpu.make_async_copy(dst, dst, rsem).wait()

    started = []

    cols = (xo, xp, xm, x)
    for k in range(NZ):
        for j in range(4):
            started.append(
                send(gp.at[at(cols[j], zk[k], oc)], rbuf.at[j, k], ps.at[j, k], pr.at[j, k], partner)
            )
    for j in range(1, NX * NC):
        started.append(send(nb1.at[xc], nb1.at[xc], ns1.at[j], nr1.at[j], xc_dev[j - 1]))

    def pair_sum(j, k):
        arrived(rbuf.at[j, k], pr.at[j, k])
        return gp[at(cols[j], zk[k], c)] + rbuf[j, k]

    right_dev, left_dev = dev(at(xp, z, c)), dev(at(xm, z, c))

    def s1(k):
        col[0, k] = pair_sum(0, k)
        started.append(send(col.at[0, k, ha], x2p.at[k], xs.at[0, k], xr.at[0, k], right_dev))
        started.append(send(col.at[0, k, hb], x2m.at[k], xs.at[1, k], xr.at[1, k], left_dev))

    def s2(k):
        col[1, k] = pair_sum(1, k)
        started.append(send(col.at[1, k, hb], left.at[k, hb], xs.at[2, k], xr.at[2, k], right_dev))
        col[2, k] = pair_sum(2, k)
        started.append(send(col.at[2, k, ha], right.at[k, ha], xs.at[3, k], xr.at[3, k], left_dev))

    def s3(k):
        arrived(x2p.at[k], xr.at[0, k])
        col[1, k, ha] = col[1, k, ha] + x2p[k]
        started.append(send(col.at[1, k, ha], left.at[k, ha], xs.at[4, k], xr.at[4, k], right_dev))
        arrived(x2m.at[k], xr.at[1, k])
        col[2, k, hb] = col[2, k, hb] + x2m[k]
        started.append(send(col.at[2, k, hb], right.at[k, hb], xs.at[5, k], xr.at[5, k], left_dev))

    def s4(k):
        own = pair_sum(3, k)
        arrived(left.at[k, hb], xr.at[2, k])
        arrived(right.at[k, ha], xr.at[3, k])
        arrived(left.at[k, ha], xr.at[4, k])
        arrived(right.at[k, hb], xr.at[5, k])
        tot[k] = own + left[k] + right[k]
        if k < NZ - 1:
            started.append(
                send(tot.at[k], zbuf.at[z], zs.at[k], zr.at[z], dev(at(x, zk[k], c)))
            )

    s1(0)
    s2(0)
    s1(1)
    s3(0)
    s2(1)
    s1(2)
    s3(1)
    s4(0)
    s2(2)
    s1(3)
    s3(2)
    s4(1)
    s2(3)

    for j in range(1, NX * NC):
        p = (xc + NX * NC - j) % (NX * NC)
        arrived(nb1.at[p], nr1.at[j])
    run = nb1[0]
    for p in range(1, NX * NC):
        run = run + nb1[p]
    nb2[z] = run
    for j in range(1, NZ):
        started.append(send(nb2.at[z], nb2.at[z], ns2.at[j], nr2.at[j], z_dev[j - 1]))

    s3(3)
    s4(2)
    s4(3)
    gsum = tot[NZ - 1]
    for j in range(1, NZ):
        p = (z + j) % NZ
        arrived(zbuf.at[p], zr.at[p])
        gsum = gsum + zbuf[p]

    one, two, update = adam_step(gsum, m1[...], m2[...], wown[...])
    dall[me] = update

    zj = [z] + [(z + j) % NZ for j in range(1, NZ)]
    for j in range(1, NZ):
        started.append(send(dall.at[me], dall.at[me], gzs.at[j], gzr.at[j], z_dev[j - 1]))

    def spread(j):
        d = at(x, zj_here[j], c)
        if j > 0:
            arrived(dall.at[d], gzr.at[src_j[j]])
        started.append(send(dall.at[d], dall.at[d], gxs.at[0, j], gxr.at[0, j], right_dev))
        started.append(send(dall.at[d], dall.at[d], gxs.at[1, j], gxr.at[1, j], left_dev))
        started.append(send(dall.at[d], dall.at[d], gps.at[0, j], gpr.at[0, j], partner))

    zj_here = [z] + [(z + NZ - j) % NZ for j in range(1, NZ)]
    src_j = [0] + list(range(1, NZ))

    def forward(j):
        dl = at(xm, zj_here[j], c)
        arrived(dall.at[dl], gxr.at[0, j])
        started.append(send(dall.at[dl, ha], dall.at[dl, ha], gxs.at[2, j], gxr.at[2, j], right_dev))
        dr = at(xp, zj_here[j], c)
        arrived(dall.at[dr], gxr.at[1, j])
        started.append(send(dall.at[dr, hb], dall.at[dr, hb], gxs.at[3, j], gxr.at[3, j], left_dev))
        started.append(send(dall.at[dl], dall.at[dl], gps.at[1, j], gpr.at[1, j], partner))
        started.append(send(dall.at[dr], dall.at[dr], gps.at[2, j], gpr.at[2, j], partner))

    def opposite(j):
        do = at(xo, zj_here[j], c)
        arrived(dall.at[do, ha], gxr.at[2, j])
        arrived(dall.at[do, hb], gxr.at[3, j])
        started.append(send(dall.at[do], dall.at[do], gps.at[3, j], gpr.at[3, j], partner))

    spread(0)

    m1n[...] = one
    m2n[...] = two
    b = idx[...]
    bounds = (0,) + matrix_bounds() + (1 << 30,)
    wsq, usq = wown[...] * wown[...], update * update
    lane = lax.broadcasted_iota(i32, (8, LANE), 1)
    row = lax.broadcasted_iota(i32, (8, LANE), 0)
    tile = jnp.zeros((8, LANE), f32)
    for k in range(MATRICES):
        inside = (b >= bounds[k]) & (b < bounds[k + 1])
        ws = jnp.sum(jnp.where(inside, wsq, 0.0), keepdims=True)
        us = jnp.sum(jnp.where(inside, usq, 0.0), keepdims=True)
        tile = tile + jnp.where((lane == k) & (row == 0), ws, 0.0)
        tile = tile + jnp.where((lane == k) & (row == 1), us, 0.0)
    sb1[xc] = tile
    for j in range(1, NX * NC):
        started.append(send(sb1.at[xc], sb1.at[xc], ss1.at[j], sr1.at[j], xc_dev[j - 1]))

    spread(1)
    forward(0)
    spread(2)
    opposite(0)

    for j in range(1, NX * NC):
        arrived(sb1.at[(xc + NX * NC - j) % (NX * NC)], sr1.at[j])
    run = sb1[0]
    for p in range(1, NX * NC):
        run = run + sb1[p]
    sb2[y] = run
    for j in range(1, ny):
        started.append(send(sb2.at[y], sb2.at[y], ss2.at[j], sr2.at[j], y_dev[j - 1]))

    forward(1)
    spread(3)

    for j in range(1, ny):
        arrived(sb2.at[(y + ny - j) % ny], sr2.at[j])
    run = sb2[0]
    for p in range(1, ny):
        run = run + sb2[p]
    sb3[zz] = run
    for j in range(1, ZH * NZ):
        started.append(send(sb3.at[zz], sb3.at[zz], ss3.at[j], sr3.at[j], zz_dev[j - 1]))

    opposite(1)
    forward(2)
    opposite(2)
    forward(3)

    for j in range(1, NZ):
        arrived(nb2.at[(z + NZ - j) % NZ], nr2.at[j])
    run = nb2[0]
    for p in range(1, NZ):
        run = run + nb2[p]
    nsum[...] = run

    for j in range(1, ZH * NZ):
        arrived(sb3.at[(zz + ZH * NZ - j) % (ZH * NZ)], sr3.at[j])
    run = sb3[0]
    for p in range(1, ZH * NZ):
        run = run + sb3[p]
    stats[...] = run

    opposite(3)

    for j in range(NZ):
        for i, x_ in enumerate((x, xm, xp, xo)):
            arrived(dall.at[at(x_, zj_here[j], oc)], gpr.at[i, j])
    for copy in started:
        copy.wait_send()


def exchange(gp, m1, m2, wown, idx, ng, ny):
    n = gp.shape[1]
    half = (n // 2 + 7) // 8 * 8
    d = ng.shape[1]
    DMA = pltpu.SemaphoreType.DMA
    chunk = (n, LANE)
    return pl.pallas_call(
        functools.partial(exchange_kernel, n, half, ny),
        out_shape=(
            jax.ShapeDtypeStruct((NX * NZ * NC, n, LANE), f32),
            jax.ShapeDtypeStruct(chunk, f32),
            jax.ShapeDtypeStruct(chunk, f32),
            jax.ShapeDtypeStruct((8, LANE), f32),
            jax.ShapeDtypeStruct((2, d), f32),
        ),
        in_specs=[pl.BlockSpec(memory_space=VMEM)] * 6,
        out_specs=(pl.BlockSpec(memory_space=VMEM),) * 5,
        scratch_shapes=[
            VMEM((4, NZ) + chunk, f32),
            VMEM((3, NZ) + chunk, f32),
            VMEM((NZ, half, LANE), f32),
            VMEM((NZ, n - half, LANE), f32),
            VMEM((NZ,) + chunk, f32),
            VMEM((NZ,) + chunk, f32),
            VMEM((NZ,) + chunk, f32),
            VMEM((NZ,) + chunk, f32),
            VMEM((NX * NC, 2, d), f32),
            VMEM((NZ, 2, d), f32),
            VMEM((NX * NC, 8, LANE), f32),
            VMEM((ny, 8, LANE), f32),
            VMEM((ZH * NZ, 8, LANE), f32),
            DMA((4, NZ)), DMA((4, NZ)),
            DMA((6, NZ)), DMA((6, NZ)),
            DMA((NZ,)), DMA((NZ,)),
            DMA((NX * NC,)), DMA((NX * NC,)),
            DMA((NZ,)), DMA((NZ,)),
            DMA((NX * NC,)), DMA((NX * NC,)),
            DMA((4,)), DMA((4,)),
            DMA((ZH * NZ,)), DMA((ZH * NZ,)),
            DMA((NZ,)), DMA((NZ,)),
            DMA((4, NZ)), DMA((4, NZ)),
            DMA((4, NZ)), DMA((4, NZ)),
        ],
        compiler_params=pltpu.CompilerParams(collective_id=0, has_side_effects=True),
        name="exchange",
    )(gp, m1, m2, wown, idx, ng)


def apply_kernel(tab, dirs, w_ref, stats, nsum, nstate, out_ref, ns_ref, trust, rows):
    step = pl.program_id(0)
    wsq = stats[0:1, :]
    usq = stats[1:2, :]
    ratio = jnp.sqrt(wsq) / (jnp.sqrt(usq) + epsilon)
    lane = lax.broadcasted_iota(i32, (1, LANE), 1)

    @pl.when(step == 0)
    def _():
        for k in range(MATRICES):
            trust[k] = jnp.sum(jnp.where(lane == k, ratio, 0.0))
        gains = nstate[0]
        one, two, update = adam_step(nsum[...], nstate[1], nstate[2], gains)
        norm_ratio = jnp.sqrt(jnp.sum(gains * gains, axis=1, keepdims=True)) / (
            jnp.sqrt(jnp.sum(update * update, axis=1, keepdims=True)) + epsilon
        )
        ns_ref[0] = gains - learning * norm_ratio * update
        ns_ref[1] = one
        ns_ref[2] = two
        which = lax.broadcasted_iota(i32, (2, 1), 0)
        for k in range(2):
            trust[MATRICES + k] = jnp.sum(jnp.where(which == k, norm_ratio, 0.0))

    base = step * RBLK
    k = jnp.int32(0)
    for bound in matrix_bounds():
        k = k + (base >= bound).astype(i32)
    rate = learning * jnp.sum(jnp.where(lane == k, ratio, 0.0), axis=1, keepdims=True)
    for r in range(RBLK):
        rows[pl.ds(r, 1), :] = dirs[pl.ds(tab[base + r], 1), :]
    out_ref[...] = w_ref[...] - rate * rows[...]


def apply(tab, dirs, weights, stats, nsum, nstate):
    total = weights.shape[0]
    whole = pl.BlockSpec(memory_space=VMEM)
    block = pl.BlockSpec((RBLK, LANE), lambda i: (i, 0))
    return pl.pallas_call(
        apply_kernel,
        out_shape=(
            jax.ShapeDtypeStruct(weights.shape, f32),
            jax.ShapeDtypeStruct(nstate.shape, f32),
            jax.ShapeDtypeStruct((MATRICES + 2,), f32),
        ),
        grid=(total // RBLK,),
        in_specs=[pl.BlockSpec(memory_space=SMEM), whole, block, whole, whole, whole],
        out_specs=(block, whole, pl.BlockSpec(memory_space=SMEM)),
        scratch_shapes=[VMEM((RBLK, LANE), f32)],
        name="new_weights",
    )(tab, dirs, weights, stats, nsum, nstate)


def local(ny, gradients, weights, first_moment, second_moment, owner_list, norm_grads, norm_state):
    total = weights.shape[0]
    n = total // (NX * NZ * NC)
    tab = tables(owner_list.reshape(total // LANE, LANE), n).reshape(-1)
    gp, wown, idx = permute(tab, gradients[0], weights, n)
    dall, m1n, m2n, stats, nsum = exchange(
        gp, first_moment[0], second_moment[0], wown, idx, norm_grads[0], ny
    )
    new_weights, new_state, trust = apply(
        tab, dall.reshape(total, LANE), weights, stats, nsum, norm_state
    )
    return new_weights, m1n[None], m2n[None], new_state, trust


def solution(mesh):
    in_specs = (
        P("dp", "mp", None),
        P("mp", None),
        P("mp", "dp", None),
        P("mp", "dp", None),
        P("mp", None),
        P("dp", None, None),
        P(),
    )
    out_specs = (P("mp", None), P("mp", "dp", None), P("mp", "dp", None), P(), P())
    return jax.shard_map(
        functools.partial(local, mesh.shape["mp"] // ZH),
        mesh=mesh, in_specs=in_specs, out_specs=out_specs, check_vma=False,
    )
```

time: 369 us -> 106 us (0.29)
  the two profiles are of different devices: /device:TPU:1 before, /device:TPU:89 now
where the time goes in v1:
time: 106 us
  Pallas kernels  102 us (96%)
  other arithmetic  1.44 us (1%)
  local copies, waits for them, and re-layouts  1.31 us (1%)
    pallas_call x1, Pallas kernels, exchange(): pl.pallas_call(functools.partial(exchange_kernel, n, half, ny), out_shape...  66.2 us
    pallas_call x1, Pallas kernels, apply(): pl.pallas_call(apply_kernel, out_shape=(jax.ShapeDtypeStruct(weights.shap...  20.9 us
    pallas_call x1, Pallas kernels, permute(): pl.pallas_call(functools.partial(permute_kernel, n), out_shape=(jax.Shape...  11.3 us
    pallas_call x1, Pallas kernels, tables(): pl.pallas_call(functools.partial(tables_kernel, n), out_shape=jax.ShapeDt...  4.02 us

profile of v1, /device:TPU:89, one launch (start us, length us, event | category | flops | bytes accessed | tf_op | source)
XLA Modules:
  0.0 105.8 jit_solution(5476323295071975226)
XLA Ops:
  0.6 1.4 %reduce = s32[7424]{0:T(1024)} reduce(s32[1,7424]{1,0:T(1,128)} %param.11, s32[]{:T(128)} %constant.5), dimensions={0}, to_apply=%param.11.reduce_sub_computation | reduce | bytes 59396 | tf_op args[4]
  2.1 4.0 %owner_tables.1 = s32[128,128]{1,0:T(8,128)} custom-call(s32[58,128]{1,0:T(8,128)} %bitcast.13), custom_call_target="tpu_custom_call" | custom-call | tf_op jit(solution)/shard_map/owner_tables/pallas_call | solution.py:88
  6.1 11.3 %permute_rows.1 = (f32[32,232,128]{2,1,0:T(8,128)}, f32[232,128]{1,0:T(8,128)}, s32[232,128]{1,0:T(8,128)}) custom-call(s32[16384]{0:T(1024)} %bitcast.11, bf16[7424,128]{1,0:T(8,128)(2,1)} %bitcast.10, f32[7424,128]{1,0:T(8,128)} %w_ref.3), custom_call_target="tpu_custom_call" | custom-call | tf_op jit(solution)/shard_map/permute_rows/pallas_call | solution.py:134
  17.4 66.2 %exchange.1 = (f32[32,232,128]{2,1,0:T(8,128)}, f32[232,128]{1,0:T(8,128)}, f32[232,128]{1,0:T(8,128)}, f32[8,128]{1,0:T(8,128)}, f32[2,1024]{1,0:T(2,128)}) custom-call(f32[32,232,128]{2,1,0:T(8,128)} %get-tuple-element.16.gp, f32[232,128]{1,0:T(8,128)} %bitcast.14, f32[232,128]{1,0:T(8,128)} %bitcast.15, f32[232,128]{1,0:T(8,128)} %get-tuple-element.17.wown, ...), custom_call_target="tpu_custom_call" | custom-call | tf_op jit(solution)/shard_map/exchange/pallas_call | solution.py:407
  83.6 0.0 copy-start.1
  83.6 0.0 copy-start
  83.6 20.9 %new_weights.1 = (f32[7424,128]{1,0:T(8,128)}, f32[3,2,1024]{2,1,0:T(2,128)}, f32[7]{0:T(128)}) custom-call(s32[16384]{0:T(1024)} %bitcast.12, f32[7424,128]{1,0:T(8,128)} %bitcast.9, f32[7424,128]{1,0:T(8,128)} %w_ref.3, f32[8,128]{1,0:T(8,128)} %get-tuple-element.20.stats, f32[2,1024]{1,0:T(2,128)} %get-tuple-element.21.nsum, f32[3,2,1024]{2,1,0:T(2,128)} %nstate.1), custom_call_target="tpu_custom_call" | custom-call | tf_op jit(solution)/shard_map/new_weights/pallas_call | solution.py:486
  104.5 0.0 copy-done.1
  104.5 0.7 copy.14
  105.1 0.0 copy-done
  105.1 0.6 copy.15
Async XLA Ops:
  83.6 20.9 %copy-start.1 = (f32[232,128]{1,0:T(8,128)S(1)}, f32[232,128]{1,0:T(8,128)}, u32[]{:S(2)}) copy-start(f32[232,128]{1,0:T(8,128)} %get-tuple-element.23) | copy-start | bytes 356356
  83.6 21.5 %copy-start = (f32[232,128]{1,0:T(8,128)S(1)}, f32[232,128]{1,0:T(8,128)}, u32[]{:S(2)}) copy-start(f32[232,128]{1,0:T(8,128)} %get-tuple-element.24) | copy-start | bytes 356356

commit v2 on v1

--- a/solution.py
+++ b/solution.py
@@ -13,6 +13,7 @@
 MATRICES = 5
 RBLK = 256
 RPAD = 256
+ORDER = 64 * LANE
 
 beta_one = 0.9
 beta_two = 0.99
@@ -44,10 +45,11 @@
 
 
 def tables_kernel(n, owner_ref, out_ref, own_s, m_s, t_s, a_s, b_s):
-    rows = owner_ref.shape[0]
+    rows = owner_ref.shape[1] // LANE
     owners = NX * NZ * NC
     own_s[...] = jnp.full((64, LANE), 99, i32)
-    own_s[0:rows, :] = owner_ref[...]
+    for i in range(rows):
+        own_s[i : i + 1, :] = owner_ref[:, i * LANE : (i + 1) * LANE]
     own = own_s[...]
     for o in range(owners):
         m_s[o * 64 : (o + 1) * 64, :] = jnp.where(own == o, 1.0, 0.0).astype(bf16)
@@ -79,12 +81,12 @@
         a_s[...], b_s[...], (((1,), (1,)), ((), ())), preferred_element_type=f32
     )
     order = (found[0:owners] * float(LANE) + found[owners:]).astype(i32)
-    out_ref[64:96, :] = order[:, :LANE]
-    out_ref[96:128, :] = order[:, LANE:]
+    out_ref[pl.ds(64, owners, stride=2), :] = order[:, :LANE]
+    out_ref[pl.ds(65, owners, stride=2), :] = order[:, LANE:]
 
 
 def tables(owner, n):
-    rows = owner.shape[0]
+    rows = owner.shape[1] // LANE
     return pl.pallas_call(
         functools.partial(tables_kernel, n),
         out_shape=jax.ShapeDtypeStruct((128, LANE), i32),
@@ -101,63 +103,16 @@
     )(owner)
 
 
-def order_at(tab, d, r):
-    return tab[(64 + (r // LANE) * 32) * LANE + d * LANE + r % LANE]
-
-
-def permute_kernel(n, tab, g_ref, w_ref, out_ref, wown_ref, idx_ref, gf):
-    total = g_ref.shape[0]
-    step = 256
-
-    def widen(i, carry):
-        at = pl.ds(pl.multiple_of(i * step, step), step)
-        gf[at, :] = g_ref[at, :].astype(f32)
-        return carry
-
-    lax.fori_loop(0, total // step, widen, 0)
-
-    def one(d, carry):
-        for r in range(n):
-            out_ref[d, pl.ds(r, 1), :] = gf[pl.ds(order_at(tab, d, r), 1), :]
-        return carry
-
-    lax.fori_loop(0, NX * NZ * NC, one, 0)
-    me = lax.axis_index("dp")
-    for r in range(n):
-        b = order_at(tab, me, r)
-        wown_ref[pl.ds(r, 1), :] = w_ref[pl.ds(b, 1), :]
-        idx_ref[pl.ds(r, 1), :] = jnp.full((1, LANE), b, i32)
-
-
-def permute(tab, grads, weights, n):
-    total = grads.shape[0]
-    return pl.pallas_call(
-        functools.partial(permute_kernel, n),
-        out_shape=(
-            jax.ShapeDtypeStruct((NX * NZ * NC, n, LANE), f32),
-            jax.ShapeDtypeStruct((n, LANE), f32),
-            jax.ShapeDtypeStruct((n, LANE), i32),
-        ),
-        in_specs=[
-            pl.BlockSpec(memory_space=SMEM),
-            pl.BlockSpec(memory_space=VMEM),
-            pl.BlockSpec(memory_space=VMEM),
-        ],
-        out_specs=(pl.BlockSpec(memory_space=VMEM),) * 3,
-        scratch_shapes=[VMEM((total, LANE), f32)],
-        name="permute_rows",
-    )(tab, grads, weights)
-
-
 def exchange_kernel(
     n, half, ny,
-    gp, m1, m2, wown, idx, ng,
+    tab, g, w_hbm, m1, m2, ng,
     dall, m1n, m2n, stats, nsum,
-    rbuf, col, x2p, x2m, left, right, zbuf, tot,
+    gf, wbuf, wown, idx,
+    pbuf, rbuf, col, x2p, x2m, left, right, zrec, tot,
     nb1, nb2, sb1, sb2, sb3,
     ps, pr, xs, xr, zs, zr,
     ns1, nr1, ns2, nr2, ss1, sr1, ss2, sr2, ss3, sr3,
-    gzs, gzr, gxs, gxr, gps, gpr,
+    gzs, gzr, gxs, gxr, gps, gpr, wsem,
 ):
     me = lax.axis_index("dp")
     m = lax.axis_index("mp")
@@ -173,8 +128,17 @@
         return x_ * (NZ * NC) + z_ * NC + c_
 
     xp, xm, xo = (x + 1) % NX, (x + 3) % NX, (x + 2) % NX
-    up = (z // 2) * 2 - 1
-    zk = [(z + up * (1 + k) + 8) % NZ for k in range(NZ)]
+    upper = z // 2
+    inner = z + upper * (NZ - 1 - 2 * z)
+
+    def mirror(v):
+        return v + upper * (NZ - 1 - 2 * v)
+
+    near = [z, mirror(1 - inner), mirror(2), mirror(3)]
+    zk = near[::-1]
+    away = 1 - 2 * upper
+    z_step = [away, away, away * (1 - 2 * inner)]
+    z_low = [(1 - v) // 2 for v in z_step]
     oc = 1 - c
     xc = x * NC + c
     xcp = [(xc + j) % (NX * NC) for j in range(1, NX * NC)]
@@ -191,11 +155,44 @@
     yp = [(y + j) % ny for j in range(1, ny)]
     y_dev = [(me, p * ZH + zh) for p in yp]
 
+    weights_in = pltpu.make_async_copy(w_hbm, wbuf, wsem)
+    weights_in.start()
     barrier = pltpu.get_barrier_semaphore()
     peers = xc_dev + zz_dev + y_dev
     for peer in peers:
         pl.semaphore_signal(barrier, inc=1, device_id=peer, device_id_type=MESH)
     nb1[xc] = ng[...].astype(f32)
+
+    def widen(i, carry):
+        rows = pl.ds(pl.multiple_of(i * 256, 256), 256)
+        gf[rows, :] = g[rows, :].astype(f32)
+        return carry
+
+    lax.fori_loop(0, g.shape[0] // 256, widen, 0)
+    unroll = n // 4
+
+    def gather(d, dst):
+        base = ORDER + d * RPAD
+
+        def body(i, carry):
+            for r in range(unroll):
+                row = i * unroll + r
+                dst[pl.ds(row, 1), :] = gf[pl.ds(tab[base + row], 1), :]
+            return carry
+
+        lax.fori_loop(0, n // unroll, body, 0)
+
+    cols = (xo, xp, xm, x)
+
+    def mine(j, k):
+        return col.at[j, k] if j < 3 else tot.at[k]
+
+    def collect(j, k):
+        gather(at(cols[j], zk[k], oc), pbuf.at[j, k])
+        gather(at(cols[j], zk[k], c), mine(j, k))
+
+    for j in range(4):
+        collect(j, 0)
     pl.semaphore_wait(barrier, len(peers))
 
     def send(src, dst, ssem, rsem, to):
@@ -211,18 +208,17 @@
 
     started = []
 
-    cols = (xo, xp, xm, x)
-    for k in range(NZ):
-        for j in range(4):
-            started.append(
-                send(gp.at[at(cols[j], zk[k], oc)], rbuf.at[j, k], ps.at[j, k], pr.at[j, k], partner)
-            )
+    def give(j, k):
+        started.append(send(pbuf.at[j, k], rbuf.at[j, k], ps.at[j, k], pr.at[j, k], partner))
+
+    for j in range(4):
+        give(j, 0)
     for j in range(1, NX * NC):
         started.append(send(nb1.at[xc], nb1.at[xc], ns1.at[j], nr1.at[j], xc_dev[j - 1]))
 
     def pair_sum(j, k):
         arrived(rbuf.at[j, k], pr.at[j, k])
-        return gp[at(cols[j], zk[k], c)] + rbuf[j, k]
+        return mine(j, k)[...] + rbuf[j, k]
 
     right_dev, left_dev = dev(at(xp, z, c)), dev(at(xm, z, c))
 
@@ -253,22 +249,45 @@
         arrived(right.at[k, hb], xr.at[5, k])
         tot[k] = own + left[k] + right[k]
         if k < NZ - 1:
-            started.append(
-                send(tot.at[k], zbuf.at[z], zs.at[k], zr.at[z], dev(at(x, zk[k], c)))
-            )
-
+            pl.when(inner == 0)(functools.partial(z_send, k))
+
+    def z_send(k):
+        send(
+            tot.at[k], zrec.at[z_low[k], zk[k]], zs.at[k], zr.at[z_low[k], zk[k]],
+            dev(at(x, z + z_step[k], c)),
+        )
+
+    def z_chain(k):
+        @pl.when(inner == 1)
+        def _():
+            arrived(zrec.at[z_low[k], zk[k]], zr.at[z_low[k], zk[k]])
+            tot[k] = tot[k] + zrec[z_low[k], zk[k]]
+            z_send(k)
+
+    def more(k, js):
+        for j in js:
+            collect(j, k)
+            give(j, k)
+
+    more(1, (0, 1))
     s1(0)
     s2(0)
+    more(1, (2, 3))
     s1(1)
     s3(0)
+    more(2, (0, 1))
     s2(1)
+    more(2, (2, 3))
     s1(2)
     s3(1)
     s4(0)
+    more(3, (0, 1))
     s2(2)
+    more(3, (2, 3))
     s1(3)
     s3(2)
     s4(1)
+    z_chain(0)
     s2(3)
 
     for j in range(1, NX * NC):
@@ -283,43 +302,67 @@
 
     s3(3)
     s4(2)
+    z_chain(1)
+
+    weights_in.wait()
+    base = ORDER + me * RPAD
+
+    def own_rows(i, carry):
+        for r in range(unroll):
+            row = i * unroll + r
+            b = tab[base + row]
+            wown[pl.ds(row, 1), :] = wbuf[pl.ds(b, 1), :]
+            idx[pl.ds(row, 1), :] = jnp.full((1, LANE), b, i32)
+        return carry
+
+    lax.fori_loop(0, n // unroll, own_rows, 0)
     s4(3)
+    z_chain(2)
+
+    @pl.when(z > 0)
+    def _():
+        arrived(zrec.at[0, z], zr.at[0, z])
+        tot[NZ - 1] = tot[NZ - 1] + zrec[0, z]
+
+    @pl.when(z < NZ - 1)
+    def _():
+        arrived(zrec.at[1, z], zr.at[1, z])
+        tot[NZ - 1] = tot[NZ - 1] + zrec[1, z]
+
     gsum = tot[NZ - 1]
-    for j in range(1, NZ):
-        p = (z + j) % NZ
-        arrived(zbuf.at[p], zr.at[p])
-        gsum = gsum + zbuf[p]
 
     one, two, update = adam_step(gsum, m1[...], m2[...], wown[...])
     dall[me] = update
 
-    zj = [z] + [(z + j) % NZ for j in range(1, NZ)]
-    for j in range(1, NZ):
-        started.append(send(dall.at[me], dall.at[me], gzs.at[j], gzr.at[j], z_dev[j - 1]))
+    def z_pass(d, z_, sem, step):
+        send(dall.at[d], dall.at[d], gzs.at[sem], gzr.at[z_], dev(at(x, z + step, c)))
+
+    pl.when(z < NZ - 1)(functools.partial(z_pass, me, z, 0, 1))
+    pl.when(z > 0)(functools.partial(z_pass, me, z, 1, -1))
 
     def spread(j):
-        d = at(x, zj_here[j], c)
+        d = at(x, near[j], c)
         if j > 0:
-            arrived(dall.at[d], gzr.at[src_j[j]])
+            arrived(dall.at[d], gzr.at[near[j]])
+            pl.when(inner == 1)(
+                functools.partial(z_pass, d, near[j], 1 + j, away if j == 1 else -away)
+            )
         started.append(send(dall.at[d], dall.at[d], gxs.at[0, j], gxr.at[0, j], right_dev))
         started.append(send(dall.at[d], dall.at[d], gxs.at[1, j], gxr.at[1, j], left_dev))
         started.append(send(dall.at[d], dall.at[d], gps.at[0, j], gpr.at[0, j], partner))
 
-    zj_here = [z] + [(z + NZ - j) % NZ for j in range(1, NZ)]
-    src_j = [0] + list(range(1, NZ))
-
     def forward(j):
-        dl = at(xm, zj_here[j], c)
+        dl = at(xm, near[j], c)
         arrived(dall.at[dl], gxr.at[0, j])
         started.append(send(dall.at[dl, ha], dall.at[dl, ha], gxs.at[2, j], gxr.at[2, j], right_dev))
-        dr = at(xp, zj_here[j], c)
+        dr = at(xp, near[j], c)
         arrived(dall.at[dr], gxr.at[1, j])
         started.append(send(dall.at[dr, hb], dall.at[dr, hb], gxs.at[3, j], gxr.at[3, j], left_dev))
         started.append(send(dall.at[dl], dall.at[dl], gps.at[1, j], gpr.at[1, j], partner))
         started.append(send(dall.at[dr], dall.at[dr], gps.at[2, j], gpr.at[2, j], partner))
 
     def opposite(j):
-        do = at(xo, zj_here[j], c)
+        do = at(xo, near[j], c)
         arrived(dall.at[do, ha], gxr.at[2, j])
         arrived(dall.at[do, hb], gxr.at[3, j])
         started.append(send(dall.at[do], dall.at[do], gps.at[3, j], gpr.at[3, j], partner))
@@ -393,17 +436,28 @@
 
     for j in range(NZ):
         for i, x_ in enumerate((x, xm, xp, xo)):
-            arrived(dall.at[at(x_, zj_here[j], oc)], gpr.at[i, j])
+            arrived(dall.at[at(x_, near[j], oc)], gpr.at[i, j])
     for copy in started:
         copy.wait_send()
-
-
-def exchange(gp, m1, m2, wown, idx, ng, ny):
-    n = gp.shape[1]
+    for k in range(NZ - 1):
+        arrived(tot.at[k], zs.at[k])
+    pl.when(z < NZ - 1)(lambda: arrived(dall.at[me], gzs.at[0]))
+    pl.when(z > 0)(lambda: arrived(dall.at[me], gzs.at[1]))
+
+    @pl.when(inner == 1)
+    def _():
+        for j in range(1, NZ):
+            arrived(dall.at[me], gzs.at[1 + j])
+
+
+def exchange(tab, grads, weights, m1, m2, ng, ny):
+    n = m1.shape[0]
     half = (n // 2 + 7) // 8 * 8
+    total = grads.shape[0]
     d = ng.shape[1]
     DMA = pltpu.SemaphoreType.DMA
     chunk = (n, LANE)
+    whole = pl.BlockSpec(memory_space=VMEM)
     return pl.pallas_call(
         functools.partial(exchange_kernel, n, half, ny),
         out_shape=(
@@ -413,16 +467,24 @@
             jax.ShapeDtypeStruct((8, LANE), f32),
             jax.ShapeDtypeStruct((2, d), f32),
         ),
-        in_specs=[pl.BlockSpec(memory_space=VMEM)] * 6,
-        out_specs=(pl.BlockSpec(memory_space=VMEM),) * 5,
+        in_specs=[
+            pl.BlockSpec(memory_space=SMEM), whole, pl.BlockSpec(memory_space=pl.ANY),
+            whole, whole, whole,
+        ],
+        out_specs=(whole,) * 5,
         scratch_shapes=[
+            VMEM((total, LANE), f32),
+            VMEM((total, LANE), f32),
+            VMEM(chunk, f32),
+            VMEM(chunk, i32),
+            VMEM((4, NZ) + chunk, f32),
             VMEM((4, NZ) + chunk, f32),
             VMEM((3, NZ) + chunk, f32),
             VMEM((NZ, half, LANE), f32),
             VMEM((NZ, n - half, LANE), f32),
             VMEM((NZ,) + chunk, f32),
             VMEM((NZ,) + chunk, f32),
-            VMEM((NZ,) + chunk, f32),
+            VMEM((2, NZ) + chunk, f32),
             VMEM((NZ,) + chunk, f32),
             VMEM((NX * NC, 2, d), f32),
             VMEM((NZ, 2, d), f32),
@@ -431,83 +493,118 @@
             VMEM((ZH * NZ, 8, LANE), f32),
             DMA((4, NZ)), DMA((4, NZ)),
             DMA((6, NZ)), DMA((6, NZ)),
-            DMA((NZ,)), DMA((NZ,)),
+            DMA((NZ,)), DMA((2, NZ)),
             DMA((NX * NC,)), DMA((NX * NC,)),
             DMA((NZ,)), DMA((NZ,)),
             DMA((NX * NC,)), DMA((NX * NC,)),
             DMA((4,)), DMA((4,)),
             DMA((ZH * NZ,)), DMA((ZH * NZ,)),
-            DMA((NZ,)), DMA((NZ,)),
+            DMA((NZ + 1,)), DMA((NZ,)),
             DMA((4, NZ)), DMA((4, NZ)),
             DMA((4, NZ)), DMA((4, NZ)),
+            DMA(()),
         ],
-        compiler_params=pltpu.CompilerParams(collective_id=0, has_side_effects=True),
+        compiler_params=pltpu.CompilerParams(
+            collective_id=0, has_side_effects=True, vmem_limit_bytes=36 * 2**20
+        ),
         name="exchange",
-    )(gp, m1, m2, wown, idx, ng)
-
-
-def apply_kernel(tab, dirs, w_ref, stats, nsum, nstate, out_ref, ns_ref, trust, rows):
-    step = pl.program_id(0)
+    )(tab, grads, weights, m1, m2, ng)
+
+
+def apply_kernel(
+    tab, dirs, w_hbm, stats, nsum, nstate, m1, m2,
+    out_hbm, ns_ref, trust, m1n, m2n,
+    wbuf, obuf, wsem, osem,
+):
+    blocks = w_hbm.shape[0] // RBLK
+
+    def block(ref, i):
+        return ref.at[pl.ds(pl.multiple_of(i * RBLK, RBLK), RBLK)]
+
+    def load(i):
+        return pltpu.make_async_copy(block(w_hbm, i), block(wbuf, i), wsem.at[i])
+
+    def save(i):
+        return pltpu.make_async_copy(block(obuf, i), block(out_hbm, i), osem.at[i])
+
+    lax.fori_loop(0, blocks, lambda i, carry: (load(i).start(), carry)[1], 0)
+
     wsq = stats[0:1, :]
     usq = stats[1:2, :]
     ratio = jnp.sqrt(wsq) / (jnp.sqrt(usq) + epsilon)
     lane = lax.broadcasted_iota(i32, (1, LANE), 1)
 
-    @pl.when(step == 0)
-    def _():
-        for k in range(MATRICES):
-            trust[k] = jnp.sum(jnp.where(lane == k, ratio, 0.0))
-        gains = nstate[0]
-        one, two, update = adam_step(nsum[...], nstate[1], nstate[2], gains)
-        norm_ratio = jnp.sqrt(jnp.sum(gains * gains, axis=1, keepdims=True)) / (
-            jnp.sqrt(jnp.sum(update * update, axis=1, keepdims=True)) + epsilon
-        )
-        ns_ref[0] = gains - learning * norm_ratio * update
-        ns_ref[1] = one
-        ns_ref[2] = two
-        which = lax.broadcasted_iota(i32, (2, 1), 0)
-        for k in range(2):
-            trust[MATRICES + k] = jnp.sum(jnp.where(which == k, norm_ratio, 0.0))
-
-    base = step * RBLK
-    k = jnp.int32(0)
-    for bound in matrix_bounds():
-        k = k + (base >= bound).astype(i32)
-    rate = learning * jnp.sum(jnp.where(lane == k, ratio, 0.0), axis=1, keepdims=True)
-    for r in range(RBLK):
-        rows[pl.ds(r, 1), :] = dirs[pl.ds(tab[base + r], 1), :]
-    out_ref[...] = w_ref[...] - rate * rows[...]
-
-
-def apply(tab, dirs, weights, stats, nsum, nstate):
+    def weigh(i, carry):
+        base = i * RBLK
+        for r in range(RBLK):
+            obuf[pl.ds(base + r, 1), :] = dirs[pl.ds(tab[base + r], 1), :]
+        k = jnp.int32(0)
+        for bound in matrix_bounds():
+            k = k + (base >= bound).astype(i32)
+        rate = learning * jnp.sum(jnp.where(lane == k, ratio, 0.0), axis=1, keepdims=True)
+        load(i).wait()
+        at = pl.ds(pl.multiple_of(base, RBLK), RBLK)
+        obuf[at, :] = wbuf[at, :] - rate * obuf[at, :]
+        save(i).start()
+        return carry
+
+    lax.fori_loop(0, blocks, weigh, 0)
+
+    m1n[...] = m1[...]
+    m2n[...] = m2[...]
+    for k in range(MATRICES):
+        trust[k] = jnp.sum(jnp.where(lane == k, ratio, 0.0))
+    gains = nstate[0]
+    one, two, update = adam_step(nsum[...], nstate[1], nstate[2], gains)
+    norm_ratio = jnp.sqrt(jnp.sum(gains * gains, axis=1, keepdims=True)) / (
+        jnp.sqrt(jnp.sum(update * update, axis=1, keepdims=True)) + epsilon
+    )
+    ns_ref[0] = gains - learning * norm_ratio * update
+    ns_ref[1] = one
+    ns_ref[2] = two
+    which = lax.broadcasted_iota(i32, (2, 1), 0)
+    for k in range(2):
+        trust[MATRICES + k] = jnp.sum(jnp.where(which == k, norm_ratio, 0.0))
+
+    lax.fori_loop(0, blocks, lambda i, carry: (save(i).wait(), carry)[1], 0)
+
+
+def apply(tab, dirs, weights, stats, nsum, nstate, m1, m2):
     total = weights.shape[0]
     whole = pl.BlockSpec(memory_space=VMEM)
-    block = pl.BlockSpec((RBLK, LANE), lambda i: (i, 0))
+    scalars = pl.BlockSpec(memory_space=SMEM)
+    place = pl.BlockSpec(memory_space=pl.ANY)
     return pl.pallas_call(
         apply_kernel,
         out_shape=(
             jax.ShapeDtypeStruct(weights.shape, f32),
             jax.ShapeDtypeStruct(nstate.shape, f32),
             jax.ShapeDtypeStruct((MATRICES + 2,), f32),
+            jax.ShapeDtypeStruct(m1.shape, f32),
+            jax.ShapeDtypeStruct(m2.shape, f32),
         ),
-        grid=(total // RBLK,),
-        in_specs=[pl.BlockSpec(memory_space=SMEM), whole, block, whole, whole, whole],
-        out_specs=(block, whole, pl.BlockSpec(memory_space=SMEM)),
-        scratch_shapes=[VMEM((RBLK, LANE), f32)],
+        in_specs=[scalars, whole, place, whole, whole, whole, whole, whole],
+        out_specs=(place, whole, scalars, whole, whole),
+        scratch_shapes=[
+            VMEM((total, LANE), f32),
+            VMEM((total, LANE), f32),
+            pltpu.SemaphoreType.DMA((total // RBLK,)),
+            pltpu.SemaphoreType.DMA((total // RBLK,)),
+        ],
+        compiler_params=pltpu.CompilerParams(vmem_limit_bytes=20 * 2**20),
         name="new_weights",
-    )(tab, dirs, weights, stats, nsum, nstate)
+    )(tab, dirs, weights, stats, nsum, nstate, m1, m2)
 
 
 def local(ny, gradients, weights, first_moment, second_moment, owner_list, norm_grads, norm_state):
     total = weights.shape[0]
     n = total // (NX * NZ * NC)
-    tab = tables(owner_list.reshape(total // LANE, LANE), n).reshape(-1)
-    gp, wown, idx = permute(tab, gradients[0], weights, n)
+    tab = tables(owner_list, n).reshape(-1)
     dall, m1n, m2n, stats, nsum = exchange(
-        gp, first_moment[0], second_moment[0], wown, idx, norm_grads[0], ny
+        tab, gradients[0], weights, first_moment[0], second_moment[0], norm_grads[0], ny
     )
-    new_weights, new_state, trust = apply(
-        tab, dall.reshape(total, LANE), weights, stats, nsum, norm_state
+    new_weights, new_state, trust, m1n, m2n = apply(
+        tab, dall.reshape(total, LANE), weights, stats, nsum, norm_state, m1n, m2n
     )
     return new_weights, m1n[None], m2n[None], new_state, trust
 

time: 106 us -> 91.2 us (0.86)
  the two profiles are of different devices: /device:TPU:89 before, /device:TPU:1 now
where the time goes in v2:
time: 91.2 us; the launch traced here: 90.9 us
  Pallas kernels  83.3 us (91%)
  local copies, waits for them, and re-layouts  6.93 us (8%)
    pallas_call x1, Pallas kernels, exchange(): pl.pallas_call(functools.partial(exchange_kernel, n, half, ny), out_shape...  62.1 us
    pallas_call x1, Pallas kernels, apply(): pl.pallas_call(apply_kernel, out_shape=(jax.ShapeDtypeStruct(weights.shap...  17.2 us
    unnamed x14, local copies, waits for them, and re-layouts  6.93 us
    pallas_call x1, Pallas kernels, tables(): pl.pallas_call(functools.partial(tables_kernel, n), out_shape=jax.ShapeDt...  4.01 us

profile of v2, /device:TPU:1, one launch (start us, length us, event | category | flops | bytes accessed | tf_op | source)
XLA Modules:
  0.0 90.9 jit_solution(5902875093533100486)
XLA Ops:
  0.6 0.0 copy-start.5
  0.6 4.0 %owner_tables.1 = s32[128,128]{1,0:T(8,128)} custom-call(s32[1,7424]{1,0:T(1,128)} %owner_ref.1), custom_call_target="tpu_custom_call" | custom-call | tf_op jit(solution)/shard_map/owner_tables/pallas_call | solution.py:90
  4.7 0.0 copy-start
  4.7 2.1 %copy-done = f32[7424,128]{1,0:T(8,128)S(1)} copy-done((f32[7424,128]{1,0:T(8,128)S(1)}, f32[7424,128]{1,0:T(8,128)}, u32[]{:S(2)}) %copy-start) | copy-done | bytes 3801112
  6.7 0.0 copy-start.1
  6.7 1.5 %copy-done.1 = bf16[1,7424,128]{2,1,0:T(8,128)(2,1)S(1)} copy-done((bf16[1,7424,128]{2,1,0:T(8,128)(2,1)S(1)}, bf16[1,7424,128]{2,1,0:T(8,128)(2,1)}, u32[]{:S(2)}) %copy-start.1) | copy-done | bytes 1900568
  8.2 0.0 copy-start.2
  8.3 0.8 copy-done.2
  9.1 0.0 copy-start.3
  9.1 0.9 copy-done.3
  10.0 0.0 copy-start.4
  10.0 0.9 copy-done.4
  10.9 0.0 copy-start.6
  10.9 0.7 copy-done.6
  11.6 62.1 %exchange.1 = (f32[32,232,128]{2,1,0:T(8,128)S(1)}, f32[232,128]{1,0:T(8,128)S(1)}, f32[232,128]{1,0:T(8,128)S(1)}, f32[8,128]{1,0:T(8,128)S(1)}, f32[2,1024]{1,0:T(2,128)S(1)}) custom-call(s32[16384]{0:T(1024)S(1)} %bitcast.10, bf16[7424,128]{1,0:T(8,128)(2,1)S(1)} %bitcast.9, f32[7424,128]{1,0:T(8,128)S(1)} %copy-done, f32[232,128]{1,0:T(8,128)S(1)} %bitcast.12, ...), custom_call_target="tpu_custom_call" | custom-call | tf_op jit(solution)/shard_map/exchange/pallas_call | solution.py:461
  73.6 0.0 copy-done.5
  73.7 17.2 %new_weights.1 = (f32[7424,128]{1,0:T(8,128)}, f32[3,2,1024]{2,1,0:T(2,128)}, f32[7]{0:T(128)}, f32[232,128]{1,0:T(8,128)}, f32[232,128]{1,0:T(8,128)}) custom-call(s32[16384]{0:T(1024)S(1)} %bitcast.11, f32[7424,128]{1,0:T(8,128)S(1)} %bitcast.8, f32[7424,128]{1,0:T(8,128)S(1)} %copy-done, f32[8,128]{1,0:T(8,128)S(1)} %get-tuple-element.16.stats, ...), custom_call_target="tpu_custom_call" | custom-call | tf_op jit(solution)/shard_map/new_weights/pallas_call | solution.py:577
Async XLA Ops:
  0.6 73.0 %copy-start.5 = (f32[3,2,1024]{2,1,0:T(2,128)S(1)}, f32[3,2,1024]{2,1,0:T(2,128)}, u32[]{:S(2)}) copy-start(f32[3,2,1024]{2,1,0:T(2,128)} %nstate.1) | copy-start | bytes 73732
  4.7 2.1 %copy-start = (f32[7424,128]{1,0:T(8,128)S(1)}, f32[7424,128]{1,0:T(8,128)}, u32[]{:S(2)}) copy-start(f32[7424,128]{1,0:T(8,128)} %w_hbm.3) | copy-start | bytes 11403268
  6.7 1.5 %copy-start.1 = (bf16[1,7424,128]{2,1,0:T(8,128)(2,1)S(1)}, bf16[1,7424,128]{2,1,0:T(8,128)(2,1)}, u32[]{:S(2)}) copy-start(bf16[1,7424,128]{2,1,0:T(8,128)(2,1)} %param.7) | copy-start | bytes 5701636
  8.2 0.8 copy-start.2
  9.1 0.9 copy-start.3
  10.0 0.9 copy-start.4
  10.9 0.7 copy-start.6
